TPU v7x, 32 devices: a whole 2x2x4 slice. The times are simulated.
32 devices in a mesh: section: 2 (over x), head: 4 (over y, core), tok: 4 (over z).
Axes of the slice: x: 2, y: 2, z: 4, core: 2. Of those that a mesh axis runs over, the one named last changes fastest.
Arguments:
- held_cotangents: bfloat16 [2, 2, 512, 2560], P('section', None, 'tok', 'head'), may hold values from -6 to 6
- entering_adjoint: bfloat16 [512, 2560], P('tok', 'head'), may hold values from -6 to 6
- saved_queries: bfloat16 [2, 512, 2560], P('section', 'tok', 'head'), may hold values from -1024 to 1024
- saved_keys: bfloat16 [2, 512, 2560], P('section', 'tok', 'head'), may hold values from -20 to 20
- value_weight: bfloat16 [2, 2560, 2560], P('section', None, 'head'), may hold values from -0.125 to 0.125
- out_weight: bfloat16 [2, 2560, 2560], P('section', 'tok', 'head'), may hold values from -0.125 to 0.125
- block_gate: float32 [2, 2560], P('section'), may hold values from -3 to 3
- time_gate: float32 [32, 2560], replicated, may hold values from -3 to 3
- timestep: int32 [1], replicated, may hold values from 0 to 31
Outputs:
- passed: bfloat16 [2, 2, 512, 2560], P('section', None, 'tok', 'head')
All inputs are finite; a program needn't handle non-finite values.
Results may differ from a plain program's by a relative error of at most 0.0085.
Values may be sent and summed in bfloat16 or wider, within the bound.
No kernel may reach another device: no remote copies, remote signals or barrier semaphores. Data moves between devices by JAX's collectives and lax.ppermute only.
A program may use at most 64 MiB of HBM per device.

v0:
```python
import jax
import jax.numpy as jnp
from jax import lax
from jax.sharding import PartitionSpec as P

HD = 128
GUIDE = 3.0


def combined_all(part, axis, combine):
    gathered = jax.tree.map(lambda a: lax.all_gather(a, axis), part)

    def take(source):
        return jax.tree.map(lambda a: lax.dynamic_index_in_dim(a, source, 0, False), gathered)

    return lax.fori_loop(
        1, lax.axis_size(axis), lambda source, state: combine(state, take(source)), take(0)
    )


def shifted(value, axis, steps):
    count = lax.axis_size(axis)
    leading, last = (max(0, -steps), min(count, count - steps))
    return lax.ppermute(value, axis, [(source, source + steps) for source in range(leading, last)])


def merge_stats(earlier, latter):
    row_top = jnp.maximum(earlier[0], latter[0])
    total_sum = earlier[1] * jnp.exp(earlier[0] - row_top) + latter[1] * jnp.exp(
        latter[0] - row_top
    )
    return (row_top, total_sum)


def body(
    held_cotangents,
    entering_adjoint,
    saved_queries,
    saved_keys,
    value_weight,
    out_weight,
    block_gate,
    time_gate,
    timestep,
):
    steps_index = jnp.arange(time_gate.shape[0])
    time_row = jnp.sum(
        jnp.where((steps_index == timestep[0])[:, None], time_gate, jnp.zeros_like(time_gate)),
        axis=0,
    )
    gate_row = block_gate[0] + time_row
    whole_cot = lax.all_gather(held_cotangents[0], "head", axis=2, tiled=True)
    scaled = (whole_cot.astype(jnp.float32) * gate_row).astype(jnp.bfloat16)
    out_full = lax.all_gather(out_weight[0], "tok", axis=0, tiled=True)
    attn_grad = jnp.einsum(
        "btd,dk->btk", scaled, out_full, preferred_element_type=jnp.float32
    ).astype(jnp.bfloat16)
    rows_here = saved_queries.shape[1]
    groups_here = saved_queries.shape[2] // HD
    score_scale = HD ** (-0.5)
    normal_grad = attn_grad[0]
    query_all = lax.all_gather(saved_queries[0], "tok", axis=0, tiled=True)
    total_rows = query_all.shape[0]
    shards = total_rows // rows_here
    key_heads = saved_keys[0].reshape(rows_here, groups_here, HD)
    scores = (
        jnp.einsum(
            "ihe,jhe->hij",
            query_all.reshape(total_rows, groups_here, HD),
            key_heads,
            preferred_element_type=jnp.float32,
        )
        * score_scale
    )
    row_top = jnp.max(scores, axis=2)
    partial_total = jnp.sum(jnp.exp(scores - row_top[:, :, None]), axis=2)
    top_all, total_all = combined_all((row_top, partial_total), "tok", merge_stats)
    log_total = top_all + jnp.log(total_all)
    weights = jnp.exp(scores - log_total[:, :, None]).astype(jnp.bfloat16)
    grad_all = lax.all_gather(normal_grad, "tok", axis=0, tiled=True)
    blocked = jnp.einsum(
        "hbij,bihe->bjhe",
        weights.reshape(groups_here, shards, rows_here, rows_here),
        grad_all.reshape(shards, rows_here, groups_here, HD),
        preferred_element_type=jnp.float32,
    )
    blocked = lax.optimization_barrier(blocked.astype(jnp.bfloat16))
    value_grad = (
        jnp.sum(blocked.astype(jnp.float32), axis=0)
        .reshape(rows_here, groups_here * HD)
        .astype(jnp.bfloat16)
    )
    stacked = jnp.stack([value_grad, attn_grad[1]])
    partial_back = jnp.einsum(
        "btk,dk->btd", stacked, value_weight[0], preferred_element_type=jnp.float32
    )
    back_sum = lax.psum_scatter(
        partial_back.astype(jnp.bfloat16), "head", scatter_dimension=2, tiled=True
    ).astype(jnp.float32)
    block_cot = (held_cotangents[0].astype(jnp.float32) + back_sum).astype(jnp.bfloat16)
    passed_on = shifted(block_cot, "section", -1)
    entering_full = entering_adjoint.astype(jnp.float32)
    fresh_rows = jnp.stack([(1.0 + GUIDE) * entering_full, -GUIDE * entering_full]).astype(
        jnp.bfloat16
    )
    is_last = lax.axis_index("section") == lax.axis_size("section") - 1
    return jnp.where(is_last, fresh_rows, passed_on)[None]


def solution(mesh):
    return jax.shard_map(
        body,
        mesh=mesh,
        in_specs=(
            P("section", None, "tok", "head"),
            P("tok", "head"),
            P("section", "tok", "head"),
            P("section", "tok", "head"),
            P("section", None, "head"),
            P("section", "tok", "head"),
            P("section", None),
            P(),
            P(),
        ),
        out_specs=P("section", None, "tok", "head"),
        check_vma=False,
    )
```

profile of v0, /device:TPU:0, one launch (start us, length us, event | category | flops | bytes accessed | tf_op | source)
XLA Modules:
  0.0 187.7 jit_solution(18396355772146746361)
XLA Ops:
  8.7 1.7 copy.22
  10.4 1.1 copy.23
  11.6 1.1 select_reduce_fusion
  12.7 19.1 %all-gather.3 = bf16[1,512,640]{1,2,0:T(8,128)(2,1)S(1)} all-gather(bf16[1,128,640]{1,2,0:T(8,128)(2,1)} %copy.22), channel_id=5, replica_groups=mesh['section'=2,'head'=4,'tok'=4] {'tok'}, dimensions={1}, use_global_device_ids=true | all-gather | bytes 819200 | tf_op jit(solution)/shard_map/all_gather | solution.py:62
  32.4 13.4 %all-gather.6 = f32[4,5,512]{2,1,0:T(8,128)S(1)} all-gather(f32[1,5,512]{2,1,0:T(8,128)S(1)} %bitcast.70), channel_id=6, replica_groups=mesh['section'=2,'head'=4,'tok'=4] {'tok'}, dimensions={0}, use_global_device_ids=true | all-gather | bytes 51200 | tf_op jit(solution)/shard_map/all_gather | solution.py:11
  46.6 14.1 %all-gather.7 = f32[4,5,512]{2,1,0:T(8,128)S(1)} all-gather(f32[1,5,512]{2,1,0:T(8,128)S(1)} %bitcast.71), channel_id=7, replica_groups=mesh['section'=2,'head'=4,'tok'=4] {'tok'}, dimensions={0}, use_global_device_ids=true | all-gather | bytes 51200 | tf_op jit(solution)/shard_map/all_gather | solution.py:11
  60.9 2.6 %exponential_convert_fusion = bf16[5,512,128]{2,1,0:T(8,128)(2,1)} fusion(f32[5,512,128]{2,1,0:T(8,128)} %copy-done.1, f32[5,512]{1,0:T(8,128)S(1)} %log_add_fusion), kind=kLoop, calls=%fused_computation.15 | loop fusion | flops 655360 | bytes 1976320 | tf_op jit(solution)/shard_map/convert_element_type | solution.py:79
  63.4 34.6 %all-gather.13.cloned.1.call-done = bf16[1,2560,640]{2,1,0:T(8,128)(2,1)} async-done(((bf16[1,640,640]{2,1,0:T(8,128)(2,1)}), bf16[1,2560,640]{2,1,0:T(8,128)(2,1)}) %all-gather.13.cloned.1.call-update) | async-done | bytes 3276816 | tf_op jit(solution)/shard_map/all_gather | solution.py:54
  98.0 3.5 %fusion.10 = bf16[2,128,640]{2,1,0:T(8,128)(2,1)S(1)} fusion(bf16[1,2560,640]{2,1,0:T(8,128)(2,1)} %all-gather.13.cloned.1.call-done, bf16[1,2,128,2560]{3,2,1,0:T(8,128)(2,1)} %all-gather.11.cloned.1.call-done, f32[2560]{0:T(1024)S(1)} %add.62), kind=kOutput, calls=%fused_computation.19 | convolution fusion | flops 840990720 | bytes 4925440 | tf_op jit(solution)/shard_map/btd,dk->btk/dot_general | solution.py:55
  102.3 17.6 %all-gather.2 = bf16[1,512,640]{2,1,0:T(8,128)(2,1)} all-gather(bf16[1,128,640]{2,1,0:T(8,128)(2,1)S(1)} %get-tuple-element.152), channel_id=4, replica_groups=mesh['section'=2,'head'=4,'tok'=4] {'tok'}, dimensions={1}, use_global_device_ids=true | all-gather | bytes 819200 | tf_op jit(solution)/shard_map/all_gather | solution.py:80
  119.9 2.5 %reshape.61 = bf16[4,128,5,128]{3,2,1,0:T(8,128)(2,1)} reshape(bf16[1,512,640]{2,1,0:T(8,128)(2,1)} %all-gather.2) | data formatting | bytes 1310720 | tf_op jit(solution)/shard_map/reshape | solution.py:84
  122.4 2.7 %fusion.9 = bf16[4,128,5,128]{1,3,2,0:T(8,128)(2,1)} fusion(bf16[4,128,5,128]{3,2,1,0:T(8,128)(2,1)} %reshape.61, bf16[5,4,128,128]{3,2,1,0:T(8,128)(2,1)} %bitcast.66), kind=kOutput, calls=%fused_computation.18 | convolution fusion | flops 84213760 | bytes 1966080 | tf_op jit(solution)/shard_map/hbij,bihe->bjhe/dot_general | solution.py:81
  125.1 1.2 reduce_sum.32
  126.3 0.8 copy.28
  127.1 3.3 %convolution_convert_fusion = bf16[2,128,2560]{2,1,0:T(8,128)(2,1)} fusion(bf16[1,2560,640]{2,1,0:T(8,128)(2,1)S(1)} %copy-done, bf16[1,128,640]{2,1,0:T(8,128)(2,1)} %get-tuple-element.153, bf16[1,128,640]{2,1,0:T(8,128)(2,1)} %copy.28), kind=kOutput, calls=%fused_computation.5 | convolution fusion | flops 839680000 | bytes 4915200 | tf_op jit(solution)/shard_map/btk,dk->btd/dot_general | solution.py:94
  130.4 4.3 %copy.33 = bf16[2,128,2560]{1,0,2:T(2,128)(2,1)} copy(bf16[2,128,2560]{2,1,0:T(8,128)(2,1)} %convolution_convert_fusion) | data formatting | bytes 2621440
  134.7 2.6 %copy.41 = bf16[320,8,2,128]{3,1,2,0:T(8,128)(2,1)} copy(bf16[320,8,2,128]{3,2,1,0:T(2,128)(2,1)} %bitcast.64) | data formatting | bytes 2621440
  137.3 25.1 %reduce-scatter.4.cloned.1.call-done = bf16[640,256]{1,0:T(8,128)(2,1)} async-done(((bf16[2560,256]{1,0:T(8,128)(2,1)}), bf16[640,256]{1,0:T(8,128)(2,1)}) %reduce-scatter.4.cloned.1.call-update) | async-done | bytes 327696
  162.4 1.8 reshape.63
  164.1 1.9 %copy.34 = bf16[2,128,640]{2,1,0:T(8,128)(2,1)} copy(bf16[2,128,640]{1,0,2:T(2,128)(2,1)} %bitcast.67) | data formatting | bytes 655360
  166.1 1.9 fusion.15
  167.9 1.3 collective-permute-start
  169.3 10.1 %collective-permute-done = bf16[2,128,640]{2,1,0:T(8,128)(2,1)} collective-permute-done((bf16[2,128,640]{2,1,0:T(8,128)(2,1)}, bf16[2,128,640]{2,1,0:T(8,128)(2,1)}, u32[]{:S(2)}, u32[]{:S(2)}) %collective-permute-start) | collective-permute-done | bytes 327712 | tf_op jit(solution)/shard_map/ppermute | solution.py:24
  179.4 1.7 fusion.20
  (29 shorter events, 3.9 us)
Async XLA Ops:
  6.5 120.6 %copy-start = (bf16[1,2560,640]{2,1,0:T(8,128)(2,1)S(1)}, bf16[1,2560,640]{2,1,0:T(8,128)(2,1)}, u32[]{:S(2)}) copy-start(bf16[1,2560,640]{2,1,0:T(8,128)(2,1)} %param.15) | copy-start | bytes 9830404
  6.5 5.0 %copy-start.3 = (f32[1,2560]{1,0:T(1,128)S(1)}, f32[1,2560]{1,0:T(1,128)}, u32[]{:S(2)}) copy-start(f32[1,2560]{1,0:T(1,128)} %param.17) | copy-start | bytes 30724
  6.5 56.9 %all-gather.11.cloned.1.call-start = ((), (), s32[]{:S(2)}) async-start(), calls=%async_computation.1 | async-start | bytes 1638400 | tf_op jit(solution)/shard_map/all_gather | solution.py:52
  7.3 90.8 %all-gather.13.cloned.1.call-start = ((), (), s32[]{:S(2)}) async-start(), calls=%async_computation.2 | async-start | bytes 4096000 | tf_op jit(solution)/shard_map/all_gather | solution.py:54
  8.0 154.4 %reduce-scatter.4.cloned.1.call-start = ((), (), s32[]{:S(2)}) async-start(), calls=%async_computation.3 | async-start | bytes 1638400
  32.4 13.4 %copy-start.1 = (f32[5,512,128]{2,1,0:T(8,128)}, f32[5,512,128]{2,1,0:T(8,128)S(1)}, u32[]{:S(2)}) copy-start(f32[5,512,128]{2,1,0:T(8,128)S(1)} %get-tuple-element.157) | copy-start | bytes 3932164
  137.3 32.0 %copy-start.2 = (bf16[128,640]{1,0:T(8,128)(2,1)S(1)}, bf16[128,640]{1,0:T(8,128)(2,1)}, u32[]{:S(2)}) copy-start(bf16[128,640]{1,0:T(8,128)(2,1)} %param.12) | copy-start | bytes 491524
  167.9 11.5 %collective-permute-start = (bf16[2,128,640]{2,1,0:T(8,128)(2,1)}, bf16[2,128,640]{2,1,0:T(8,128)(2,1)}, u32[]{:S(2)}, u32[]{:S(2)}) collective-permute-start(bf16[2,128,640]{2,1,0:T(8,128)(2,1)} %fusion.15), channel_id=1, source_target_pairs={{16,0},{17,1},{18,2},{19,3},{20,4},{21,5},{22,6},{23,7},{24,8},{25... | collective-permute-start | bytes 983048 | tf_op jit(solution)/shard_map/ppermute | solution.py:24
Sparse Core Ops, SparseCore 0:
  8.9 20.8 all-gather.10
  31.4 66.6 all-gather.12
  137.4 24.9 reduce-scatter.3
where the time goes:
time: 188 us
  waiting for transfers between devices  71.2 us (38%)
  blocking collectives  64.3 us (34%)
  local copies, waits for them, and re-layouts  17.4 us (9%)
  between operations  13.9 us (7%)
  matrix products  10.1 us (5%)
  other arithmetic  9.44 us (5%)
    all_gather x1, waiting for transfers between devices, body(): out_full = lax.all_gather(out_weight[0], 'tok', axis=0, tiled=True)  34.6 us
    all_gather x2, blocking collectives, combined_all(): gathered = jax.tree.map(lambda a: lax.all_gather(a, axis), part)  27.5 us
    unnamed x4, waiting for transfers between devices  26.5 us
    all_gather x1, blocking collectives, body(): query_all = lax.all_gather(saved_queries[0], 'tok', axis=0, tiled=True)  19.1 us
    all_gather x1, blocking collectives, body(): grad_all = lax.all_gather(normal_grad, 'tok', axis=0, tiled=True)  17.6 us
    unnamed x14, local copies, waits for them, and re-layouts  13.3 us
    ppermute x1, waiting for transfers between devices, shifted(): lax.ppermute(value, axis, [(source, source + steps) for source in range(l...  10.1 us
  transfers between devices with their start and end apart: 4, of which 3 were waited for; matrix products, arithmetic and copies ran while one was open for 4% of the time, Pallas kernels for 0%

commit v1 on v0

--- a/solution.py
+++ b/solution.py
@@ -77,7 +77,14 @@
     top_all, total_all = combined_all((row_top, partial_total), "tok", merge_stats)
     log_total = top_all + jnp.log(total_all)
     weights = jnp.exp(scores - log_total[:, :, None]).astype(jnp.bfloat16)
-    grad_all = lax.all_gather(normal_grad, "tok", axis=0, tiled=True)
+    peers = lax.axis_size("tok")
+    hops = [(i, (i + 1) % peers) for i in range(peers)]
+    pieces = [normal_grad]
+    for hop in range(1, peers):
+        pieces = [lax.ppermute(pieces[0], "tok", hops), *pieces]
+    whole = jnp.concatenate(pieces, axis=0)
+    shift = (lax.axis_index("tok") + 1) * pieces[-1].shape[0]
+    grad_all = jnp.roll(whole, shift, axis=0)
     blocked = jnp.einsum(
         "hbij,bihe->bjhe",
         weights.reshape(groups_here, shards, rows_here, rows_here),

time: 188 us -> 195 us (1.037)
  waiting for transfers between devices: 71.2 us -> 90.8 us
  blocking collectives: 64.3 us -> 46.6 us
  other arithmetic: 9.44 us -> 11.6 us
    all_gather x1 -> x0, blocking collectives: 17.6 us -> none  [body(): grad_all = lax.all_gather(normal_grad, 'tok', axis=0, tiled=True)]
    ppermute x0 -> x3, waiting for transfers between devices: none -> 17.1 us  [body(): pieces = [lax.ppermute(pieces[0], 'tok', hops), *pieces]]
    all_gather x1, waiting for transfers between devices: 34.6 us -> 37.3 us  [body(): out_full = lax.all_gather(out_weight[0], 'tok', axis=0, tiled=True)]
    add x3, other arithmetic: 0.06 us -> 2.22 us  [merge_stats(): earlier[1] * jnp.exp(earlier[0] - row_top)]
    unnamed x14 -> x27, local copies, waits for them, and re-layouts: 13.3 us -> 14.2 us
  transfers between devices with their start and end apart: 4 -> 7, of which waited for: 3 -> 6; matrix products, arithmetic and copies ran while one was open for 4% -> 5% of each run, Pallas kernels for 0% -> 0%
where the time goes in v1:
time: 195 us; the launch traced here: 194 us
  waiting for transfers between devices  90.8 us (47%)
  blocking collectives  46.6 us (24%)
  local copies, waits for them, and re-layouts  19.3 us (10%)
  between operations  14 us (7%)
  other arithmetic  11.6 us (6%)
  matrix products  10.1 us (5%)
    all_gather x1, waiting for transfers between devices, body(): out_full = lax.all_gather(out_weight[0], 'tok', axis=0, tiled=True)  37.3 us
    all_gather x2, blocking collectives, combined_all(): gathered = jax.tree.map(lambda a: lax.all_gather(a, axis), part)  27.5 us
    unnamed x4, waiting for transfers between devices  26.2 us
    all_gather x1, blocking collectives, body(): query_all = lax.all_gather(saved_queries[0], 'tok', axis=0, tiled=True)  19.1 us
    ppermute x3, waiting for transfers between devices, body(): pieces = [lax.ppermute(pieces[0], 'tok', hops), *pieces]  17.1 us
    unnamed x27, local copies, waits for them, and re-layouts  14.2 us
    ppermute x1, waiting for transfers between devices, shifted(): lax.ppermute(value, axis, [(source, source + steps) for source in range(l...  10.1 us
  transfers between devices with their start and end apart: 7, of which 6 were waited for; matrix products, arithmetic and copies ran while one was open for 5% of the time, Pallas kernels for 0%

profile of v1, /device:TPU:0, one launch (start us, length us, event | category | flops | bytes accessed | tf_op | source)
XLA Modules:
  0.0 193.8 jit_solution(16527352367496950164)
XLA Ops:
  8.7 1.7 copy.21
  12.7 19.1 %all-gather.2 = bf16[1,512,640]{1,2,0:T(8,128)(2,1)S(1)} all-gather(bf16[1,128,640]{1,2,0:T(8,128)(2,1)} %copy.21), channel_id=4, replica_groups=mesh['section'=2,'head'=4,'tok'=4] {'tok'}, dimensions={1}, use_global_device_ids=true | all-gather | bytes 819200 | tf_op jit(solution)/shard_map/all_gather | solution.py:62
  32.4 13.4 %all-gather.5 = f32[4,5,512]{2,1,0:T(8,128)S(1)} all-gather(f32[1,5,512]{2,1,0:T(8,128)S(1)} %bitcast.76), channel_id=5, replica_groups=mesh['section'=2,'head'=4,'tok'=4] {'tok'}, dimensions={0}, use_global_device_ids=true | all-gather | bytes 51200 | tf_op jit(solution)/shard_map/all_gather | solution.py:11
  46.6 14.1 %all-gather.6 = f32[4,5,512]{2,1,0:T(8,128)S(1)} all-gather(f32[1,5,512]{2,1,0:T(8,128)S(1)} %bitcast.77), channel_id=6, replica_groups=mesh['section'=2,'head'=4,'tok'=4] {'tok'}, dimensions={0}, use_global_device_ids=true | all-gather | bytes 51200 | tf_op jit(solution)/shard_map/all_gather | solution.py:11
  60.7 37.3 %all-gather.12.cloned.1.call-done = bf16[1,2560,640]{2,1,0:T(8,128)(2,1)} async-done(((bf16[1,640,640]{2,1,0:T(8,128)(2,1)}), bf16[1,2560,640]{2,1,0:T(8,128)(2,1)}) %all-gather.12.cloned.1.call-update) | async-done | bytes 3276816 | tf_op jit(solution)/shard_map/all_gather | solution.py:54
  98.0 3.5 %fusion.10 = bf16[2,128,640]{2,1,0:T(8,128)(2,1)S(1)} fusion(bf16[1,2560,640]{2,1,0:T(8,128)(2,1)} %all-gather.12.cloned.1.call-done, bf16[1,2,128,2560]{3,2,1,0:T(8,128)(2,1)} %all-gather.10.cloned.1.call-done, f32[2560]{0:T(1024)S(1)} %add.75), kind=kOutput, calls=%fused_computation.19 | convolution fusion | flops 840990720 | bytes 4925440 | tf_op jit(solution)/shard_map/btd,dk->btk/dot_general | solution.py:55
  103.1 2.3 %while.17 = (s32[]{:T(128)}, f32[5,512]{1,0:T(8,128)S(1)}, f32[5,512]{1,0:T(8,128)S(1)}, f32[4,5,512]{2,1,0:T(8,128)S(1)}, f32[4,5,512]{2,1,0:T(8,128)}, /*index=5*/s32[]{:T(128)}, s32[]{:T(128)}, s32[]{:T(128)}) while((s32[]{:T(128)}, f32[5,512]{1,0:T(8,128)S(1)}, f32[5,512]{1,0:T(8,128)S(1)}, f32[4,5,512]{2,1,0:T(8,128)S(1)}, ...), condition=%wide.region_4.5_spmd, body=%wide.region_3.4_spmd.sunk | while | flops 15365 | bytes 61571 | solution.py:16
  105.4 5.6 %collective-permute-done = bf16[128,640]{1,0:T(8,128)(2,1)S(1)} collective-permute-done((bf16[128,640]{1,0:T(8,128)(2,1)}, bf16[128,640]{1,0:T(8,128)(2,1)S(1)}, u32[]{:S(2)}, u32[]{:S(2)}) %collective-permute-start) | collective-permute-done | bytes 163872 | tf_op jit(solution)/shard_map/ppermute | solution.py:84
  110.9 7.1 %collective-permute-done.1 = bf16[128,640]{1,0:T(8,128)(2,1)S(1)} collective-permute-done((bf16[128,640]{1,0:T(8,128)(2,1)S(1)}, bf16[128,640]{1,0:T(8,128)(2,1)S(1)}, u32[]{:S(2)}, u32[]{:S(2)}) %collective-permute-start.1) | collective-permute-done | bytes 163872 | tf_op jit(solution)/shard_map/ppermute | solution.py:84
  118.0 2.6 %exponential_convert_fusion = bf16[5,512,128]{2,1,0:T(8,128)(2,1)} fusion(f32[5,512,128]{2,1,0:T(8,128)} %copy-done.1, f32[5,512]{1,0:T(8,128)S(1)} %log_add_fusion), kind=kLoop, calls=%fused_computation.15 | loop fusion | flops 655360 | bytes 1976320 | tf_op jit(solution)/shard_map/convert_element_type | solution.py:79
  120.7 4.5 %collective-permute-done.2 = bf16[128,640]{1,0:T(8,128)(2,1)S(1)} collective-permute-done((bf16[128,640]{1,0:T(8,128)(2,1)S(1)}, bf16[128,640]{1,0:T(8,128)(2,1)S(1)}, u32[]{:S(2)}, u32[]{:S(2)}) %collective-permute-start.2) | collective-permute-done | bytes 163872 | tf_op jit(solution)/shard_map/ppermute | solution.py:84
  126.3 2.5 %reshape.59 = bf16[4,128,5,128]{3,2,1,0:T(8,128)(2,1)} reshape(bf16[512,640]{1,0:T(8,128)(2,1)} %constant_dynamic-slice_fusion) | data formatting | bytes 1310720 | tf_op jit(solution)/shard_map/reshape | solution.py:91
  128.8 2.6 %fusion.9 = bf16[4,128,5,128]{1,3,2,0:T(8,128)(2,1)} fusion(bf16[4,128,5,128]{3,2,1,0:T(8,128)(2,1)} %reshape.59, bf16[5,4,128,128]{3,2,1,0:T(8,128)(2,1)} %bitcast.72), kind=kOutput, calls=%fused_computation.18 | convolution fusion | flops 84213760 | bytes 1966080 | tf_op jit(solution)/shard_map/hbij,bihe->bjhe/dot_general | solution.py:88
  131.5 1.2 reduce_sum.32
  133.5 3.3 %convolution_convert_fusion = bf16[2,128,2560]{2,1,0:T(8,128)(2,1)} fusion(bf16[1,2560,640]{2,1,0:T(8,128)(2,1)S(1)} %copy-done, bf16[1,128,640]{2,1,0:T(8,128)(2,1)} %get-tuple-element.153, bf16[1,128,640]{2,1,0:T(8,128)(2,1)} %copy.27), kind=kOutput, calls=%fused_computation.5 | convolution fusion | flops 839680000 | bytes 4915200 | tf_op jit(solution)/shard_map/btk,dk->btd/dot_general | solution.py:101
  136.8 4.3 %copy.32 = bf16[2,128,2560]{1,0,2:T(2,128)(2,1)} copy(bf16[2,128,2560]{2,1,0:T(8,128)(2,1)} %convolution_convert_fusion) | data formatting | bytes 2621440
  141.1 2.6 %copy.40 = bf16[320,8,2,128]{3,1,2,0:T(8,128)(2,1)} copy(bf16[320,8,2,128]{3,2,1,0:T(2,128)(2,1)} %bitcast.70) | data formatting | bytes 2621440
  143.7 24.8 %reduce-scatter.4.cloned.1.call-done = bf16[640,256]{1,0:T(8,128)(2,1)} async-done(((bf16[2560,256]{1,0:T(8,128)(2,1)}), bf16[640,256]{1,0:T(8,128)(2,1)}) %reduce-scatter.4.cloned.1.call-update) | async-done | bytes 327696
  168.4 1.8 reshape.61
  170.2 1.9 copy.33
  172.1 1.9 fusion.15
  174.0 1.3 collective-permute-start.3
  175.4 10.1 %collective-permute-done.3 = bf16[2,128,640]{2,1,0:T(8,128)(2,1)} collective-permute-done((bf16[2,128,640]{2,1,0:T(8,128)(2,1)}, bf16[2,128,640]{2,1,0:T(8,128)(2,1)}, u32[]{:S(2)}, u32[]{:S(2)}) %collective-permute-start.3) | collective-permute-done | bytes 327712 | tf_op jit(solution)/shard_map/ppermute | solution.py:24
  185.5 1.7 fusion.20
  (49 shorter events, 10.9 us)
Async XLA Ops:
  6.5 127.0 %copy-start = (bf16[1,2560,640]{2,1,0:T(8,128)(2,1)S(1)}, bf16[1,2560,640]{2,1,0:T(8,128)(2,1)}, u32[]{:S(2)}) copy-start(bf16[1,2560,640]{2,1,0:T(8,128)(2,1)} %param.15) | copy-start | bytes 9830404
  6.5 5.0 %copy-start.6 = (f32[1,2560]{1,0:T(1,128)S(1)}, f32[1,2560]{1,0:T(1,128)}, u32[]{:S(2)}) copy-start(f32[1,2560]{1,0:T(1,128)} %param.17) | copy-start | bytes 30724
  6.5 54.2 %all-gather.10.cloned.1.call-start = ((), (), s32[]{:S(2)}) async-start(), calls=%async_computation.1 | async-start | bytes 1638400 | tf_op jit(solution)/shard_map/all_gather | solution.py:52
  7.3 90.8 %all-gather.12.cloned.1.call-start = ((), (), s32[]{:S(2)}) async-start(), calls=%async_computation.2 | async-start | bytes 4096000 | tf_op jit(solution)/shard_map/all_gather | solution.py:54
  8.0 160.4 %reduce-scatter.4.cloned.1.call-start = ((), (), s32[]{:S(2)}) async-start(), calls=%async_computation.3 | async-start | bytes 1638400
  32.4 13.4 %copy-start.1 = (f32[5,512,128]{2,1,0:T(8,128)}, f32[5,512,128]{2,1,0:T(8,128)S(1)}, u32[]{:S(2)}) copy-start(f32[5,512,128]{2,1,0:T(8,128)S(1)} %get-tuple-element.157) | copy-start | bytes 3932164
  60.7 40.9 %copy-start.4 = (f32[4,5,512]{2,1,0:T(8,128)}, f32[4,5,512]{2,1,0:T(8,128)S(1)}, u32[]{:S(2)}) copy-start(f32[4,5,512]{2,1,0:T(8,128)S(1)} %all-gather.6) | copy-start | bytes 122884
  101.6 0.7 copy-start.2
  103.1 7.8 %collective-permute-start = (bf16[128,640]{1,0:T(8,128)(2,1)}, bf16[128,640]{1,0:T(8,128)(2,1)S(1)}, u32[]{:S(2)}, u32[]{:S(2)}) collective-permute-start(bf16[128,640]{1,0:T(8,128)(2,1)} %get-tuple-element.152), channel_id=1, source_target_pairs={{0,1},{1,2},{2,3},{3,0},{4,5},{5,6},{6,7},{7,4},{8,9},{9,10},{10,1... | collective-permute-start | bytes 491528 | tf_op jit(solution)/shard_map/ppermute | solution.py:84
  110.9 7.1 %collective-permute-start.1 = (bf16[128,640]{1,0:T(8,128)(2,1)S(1)}, bf16[128,640]{1,0:T(8,128)(2,1)S(1)}, u32[]{:S(2)}, u32[]{:S(2)}) collective-permute-start(bf16[128,640]{1,0:T(8,128)(2,1)S(1)} %collective-permute-done), channel_id=1, source_target_pairs={{0,1},{1,2},{2,3},{3,0},{4,5},{5,6},{6,7},{7,4},{8,9},{9,10},{10,1... | collective-permute-start | bytes 491528 | tf_op jit(solution)/shard_map/ppermute | solution.py:84
  110.9 14.3 %copy-start.3 = (bf16[2,128,640]{2,1,0:T(8,128)(2,1)S(1)}, bf16[2,128,640]{2,1,0:T(8,128)(2,1)}, u32[]{:S(2)}) copy-start(bf16[2,128,640]{2,1,0:T(8,128)(2,1)} %copy-done.2) | copy-start | bytes 983044
  118.0 7.1 %collective-permute-start.2 = (bf16[128,640]{1,0:T(8,128)(2,1)S(1)}, bf16[128,640]{1,0:T(8,128)(2,1)S(1)}, u32[]{:S(2)}, u32[]{:S(2)}) collective-permute-start(bf16[128,640]{1,0:T(8,128)(2,1)S(1)} %collective-permute-done.1), channel_id=1, source_target_pairs={{0,1},{1,2},{2,3},{3,0},{4,5},{5,6},{6,7},{7,4},{8,9},{9,10},{10,1... | collective-permute-start | bytes 491528 | tf_op jit(solution)/shard_map/ppermute | solution.py:84
  143.7 31.6 %copy-start.5 = (bf16[128,640]{1,0:T(8,128)(2,1)S(1)}, bf16[128,640]{1,0:T(8,128)(2,1)}, u32[]{:S(2)}) copy-start(bf16[128,640]{1,0:T(8,128)(2,1)} %param.12) | copy-start | bytes 491524
  174.0 11.5 %collective-permute-start.3 = (bf16[2,128,640]{2,1,0:T(8,128)(2,1)}, bf16[2,128,640]{2,1,0:T(8,128)(2,1)}, u32[]{:S(2)}, u32[]{:S(2)}) collective-permute-start(bf16[2,128,640]{2,1,0:T(8,128)(2,1)} %fusion.15), channel_id=1, source_target_pairs={{16,0},{17,1},{18,2},{19,3},{20,4},{21,5},{22,6},{23,7},{24,8},{25... | collective-permute-start | bytes 983048 | tf_op jit(solution)/shard_map/ppermute | solution.py:24
Sparse Core Ops, SparseCore 0:
  8.9 20.8 all-gather.9
  31.4 66.6 all-gather.11
  143.8 24.6 reduce-scatter.3
